TPU v7x, 32 devices: a whole 2x2x4 slice. The times are simulated.
32 devices in a mesh: sec: 2 (over y), blk: 16 (over z, x, core).
Axes of the slice: x: 2, y: 2, z: 4, core: 2. Of those that a mesh axis runs over, the one named last changes fastest.
Arguments:
- wave_speed: float32 [2, 125, 4096], P('sec', None, 'blk'), may hold values from 0.5 to 2
- inverse_mass: float32 [2, 125, 4096], P('sec', None, 'blk'), may hold values from 0.5 to 2
- source_field: float32 [2, 125, 4096], P('sec', None, 'blk'), may hold values from -4 to 4
- source_time: float32 [2, 12], P('sec'), may hold values from -4 to 4
- face_links: int32 [2, 3, 2048], P('sec', None, 'blk'), may hold values from 0 to 255, as said below
- coupling_links: int32 [5, 8192], P(None, 'blk'), may hold values from -1 to 255, as said below
Outputs:
- adjoint_now: float32 [2, 125, 4096], P('sec', None, 'blk')
- adjoint_before: float32 [2, 125, 4096], P('sec', None, 'blk')
Inputs may be any that keep to these rules, and one draw needn't show every extreme that they name: `face_links`: in each section record k of block b and record k of its peer name each other; the peer is b XOR 2^j for a bit j that depends on the section and k only, and equals b for unlinked records, which are the trailing ones. A block's records name distinct elements. A block has at most 16 records with one peer and exactly 16 with some peer. `coupling_links`: owner -1 marks unused points, which are the trailing points of a block. A box block has at most 4 points with one owner, and every box block has exactly 4 points with one common owner.
All inputs are finite; a program needn't handle non-finite values.
Results may differ from a plain program's by a relative error of at most 0.0001.
Values sent between devices are 32-bit elements; how exact they have to be, the bound alone decides.
No kernel may reach another device: no remote copies, remote signals or barrier semaphores. Data moves between devices by JAX's collectives and lax.ppermute only.
A program may use at most 64 MiB of HBM per device.

v0:
```python
import jax
import jax.numpy as jnp
import numpy as np
from jax import lax
from jax.sharding import PartitionSpec as P

CAPC = 4
STEPS = 12
DT_SQUARED = 0.05
PENALTY = 10.0


def partner_2(value, axis, stride):
    return lax.ppermute(value, axis, [(i, i ^ 1 << stride) for i in range(lax.axis_size(axis))])


def node_tables():
    abscissae = np.array([-1.0, -np.sqrt(3.0 / 7.0), 0.0, np.sqrt(3.0 / 7.0), 1.0])
    weights = np.array([0.1, 49.0 / 90.0, 32.0 / 45.0, 49.0 / 90.0, 0.1])
    legendre = (35.0 * abscissae**4 - 30.0 * abscissae**2 + 3.0) / 8.0
    derivative = np.zeros((5, 5))
    for i in range(5):
        for j in range(5):
            if i != j:
                derivative[i, j] = legendre[i] / (legendre[j] * (abscissae[i] - abscissae[j]))
    derivative[0, 0] = -2.5
    derivative[4, 4] = 2.5
    identity = np.eye(5)
    operator = np.concatenate(
        [
            np.kron(np.kron(derivative, identity), identity),
            np.kron(np.kron(identity, derivative), identity),
            np.kron(np.kron(identity, identity), derivative),
        ],
        axis=0,
    )
    weight_cube = weights[:, None, None] * weights[None, :, None] * weights[None, None, :]
    lattice = np.arange(125).reshape(5, 5, 5)
    face_nodes = np.stack(
        [
            lattice[0].ravel(),
            lattice[4].ravel(),
            lattice[:, 0].ravel(),
            lattice[:, 4].ravel(),
            lattice[:, :, 0].ravel(),
            lattice[:, :, 4].ravel(),
        ]
    )
    return (
        operator.astype(np.float32),
        weight_cube.reshape(125, 1).astype(np.float32),
        face_nodes.astype(np.int32),
    )


def stiffness(field_in, speed_sq, operator, weight_cube):
    columns = field_in.shape[-1]
    scaling = weight_cube * speed_sq
    grads = jnp.dot(
        operator, field_in, precision=lax.Precision.HIGHEST, preferred_element_type=jnp.float32
    )
    scaled = (grads.reshape(3, 125, columns) * scaling[None]).reshape(375, columns)
    return jnp.dot(
        operator.T, scaled, precision=lax.Precision.HIGHEST, preferred_element_type=jnp.float32
    )


def body(wave_speed, inverse_mass, source_field, source_time, face_links, coupling_links):
    operator_np, weight_np, faces_np = node_tables()
    operator = jnp.asarray(operator_np)
    weight_cube = jnp.asarray(weight_np)
    picker_np = np.zeros((150, 125), np.float32)
    for side_number in range(6):
        for node_number in range(25):
            picker_np[side_number * 25 + node_number, faces_np[side_number, node_number]] = 1.0
    picker = jnp.asarray(picker_np)
    spreader = jnp.asarray(picker_np.T.copy())
    speed_sq = wave_speed[0]
    inverse = inverse_mass[0]
    forcing = source_field[0]
    timing = source_time[0]
    element = face_links[0, 0]
    face_side = face_links[0, 1]
    face_peer = face_links[0, 2]
    blocks = lax.axis_size("blk")
    bit_count = blocks.bit_length() - 1
    myself = lax.axis_index("blk")
    is_box = lax.axis_index("sec") == 0
    records = element.shape[0]
    per_peer = records // 8
    ordinal = jnp.arange(records)
    linked = face_peer != myself
    side_mask = face_side[None, None, :] == jnp.arange(6, dtype=jnp.int32)[:, None, None]
    earlier = ordinal[None, :] < ordinal[:, None]
    face_slot = jnp.sum(
        ((face_peer[:, None] == face_peer[None, :]) & earlier).astype(jnp.int32), axis=1
    )
    offset_bits = jnp.bitwise_xor(face_peer, myself)
    bit_index = jnp.zeros((records,), jnp.int32)
    for bit_number in range(bit_count):
        bit_index = bit_index + bit_number * (offset_bits == 1 << bit_number).astype(jnp.int32)
    pair_column = jnp.where(linked, bit_index * per_peer + face_slot, 0)
    point_element = coupling_links[0]
    point_node = coupling_links[1]
    point_owner = coupling_links[2]
    target_element = coupling_links[3]
    target_node = coupling_links[4]
    in_use = point_owner >= 0
    owner_safe = jnp.maximum(point_owner, 0)
    point_ordinal = jnp.arange(point_owner.shape[0])
    point_earlier = point_ordinal[None, :] < point_ordinal[:, None]
    point_slot = jnp.sum(
        ((point_owner[:, None] == point_owner[None, :]) & point_earlier).astype(jnp.int32), axis=1
    )
    point_column = jnp.where(in_use, point_slot * blocks + owner_safe, 0)
    slot_total = CAPC * blocks
    outbound = jnp.zeros((3, slot_total), jnp.int32)
    outbound = outbound.at[0, point_column].add(jnp.where(in_use, target_element, 0))
    outbound = outbound.at[1, point_column].add(jnp.where(in_use, target_node, 0))
    outbound = outbound.at[2, point_column].add(in_use.astype(jnp.int32))
    inbound = lax.all_to_all(
        outbound.reshape(3, CAPC, blocks), "blk", split_axis=2, concat_axis=2, tiled=True
    ).reshape(3, slot_total)
    remote_element = inbound[0]
    remote_node = inbound[1]
    remote_flag = inbound[2].astype(jnp.float32)
    target_rows = jnp.concatenate([point_node, remote_node])
    target_cols = jnp.concatenate([point_element, remote_element])
    current = jnp.zeros(speed_sq.shape, jnp.float32)
    previous = jnp.zeros(speed_sq.shape, jnp.float32)
    for moment in range(STEPS):
        internal = stiffness(current, speed_sq, operator, weight_cube)
        stacked = jnp.dot(
            picker,
            internal[:, element],
            precision=lax.Precision.HIGHEST,
            preferred_element_type=jnp.float32,
        ).reshape(6, 25, records)
        payload = jnp.sum(jnp.where(side_mask, stacked, 0.0), axis=0)
        payload = jnp.where(linked[None, :], payload, 0.0)
        outgoing = (
            jnp.zeros((25, bit_count * per_peer), jnp.float32).at[:, pair_column].add(payload)
        )
        arrived = []
        for bit_number in range(bit_count):
            piece = outgoing[:, bit_number * per_peer : (bit_number + 1) * per_peer]
            arrived.append(partner_2(piece, "blk", bit_number))
        partner = jnp.concatenate(arrived, axis=1)[:, pair_column]
        partner = jnp.where(linked[None, :], partner, 0.0)
        masked = jnp.where(side_mask, partner[None], 0.0).reshape(150, records)
        assembled = internal.at[:, element].add(
            jnp.dot(
                spreader,
                masked,
                precision=lax.Precision.HIGHEST,
                preferred_element_type=jnp.float32,
            )
        )
        velocity = current - previous
        traction = assembled[point_node, point_element]
        box_send = (
            jnp.zeros((slot_total,), jnp.float32)
            .at[point_column]
            .add(jnp.where(in_use, traction, 0.0))
        )
        global_send = velocity[remote_node, remote_element] * remote_flag
        dispatch = jnp.where(is_box, box_send, global_send).reshape(CAPC, blocks)
        crossed = partner_2(dispatch, "sec", 0)
        received = lax.all_to_all(crossed, "blk", split_axis=1, concat_axis=1, tiled=True)
        received = received.reshape(slot_total)
        remote_velocity = received[point_column]
        box_terms = jnp.where(
            in_use, PENALTY * (remote_velocity - velocity[point_node, point_element]), 0.0
        )
        values = jnp.concatenate(
            [jnp.where(is_box, box_terms, 0.0), jnp.where(is_box, 0.0, received * remote_flag)]
        )
        driving = timing[moment] * forcing - assembled
        driving = driving.at[target_rows, target_cols].add(values)
        advanced = 2.0 * current - previous + DT_SQUARED * inverse * driving
        previous = current
        current = advanced
    return (current[None], previous[None])


def solution(mesh):
    in_specs = (
        P("sec", None, "blk"),
        P("sec", None, "blk"),
        P("sec", None, "blk"),
        P("sec", None),
        P("sec", None, "blk"),
        P(None, "blk"),
    )
    out_specs = (P("sec", None, "blk"), P("sec", None, "blk"))
    return jax.shard_map(body, mesh=mesh, in_specs=in_specs, out_specs=out_specs, check_vma=False)
```

profile of v0, /device:TPU:0, one launch (start us, length us, event | category | flops | bytes accessed | tf_op | source)
XLA Modules:
  0.0 1408.7 jit_solution(6198110718570769417)
XLA Ops:
  128.0 40.1 %fusion.83 = (f32[512]{0:T(512)S(1)}, pred[512]{0:T(512)(128)(4,1)S(1)}, pred[512]{0:T(512)(128)(4,1)S(1)}, pred[512]{0:T(512)(128)(4,1)S(1)}, pred[512]{0:T(512...) fusion(pred[512]{0:T(512)(128)(4,1)S(1)} %get-tuple-element.99,, ...), kind=kLoop, calls=%fused_computation.341 | loop fusion | flops 66560 | bytes 39169 | tf_op jit(solution)/shard_map/jit(_where)/select_n | solution.py:176
  168.1 30.1 %scatter_fusion.4 = f32[125,256]{1,0:T(8,128)S(1)} fusion(f32[125,256]{1,0:T(8,128)S(1)} %copy.421, s32[576]{0:T(1024)S(1)} %fusion.42, f32[576]{0:T(1024)S(1)} %pad_maximum_fusion.12), kind=kCustom, calls=%fused_computation.66 | custom fusion | flops 576 | bytes 11520 | tf_op jit(solution)/shard_map/scatter-add | solution.py:179
  238.2 40.1 %fusion.80 = f32[512]{0:T(512)S(1)} fusion(pred[512]{0:T(512)(128)(4,1)S(1)} %get-tuple-element.99, f32[512]{0:T(512)S(1)} %gather_fusion.9, pred[512]{0:T(512)(128)(4,1)S(1)} %get-tuple-element.97, pred[512]{0:T(512)(128)(4,1)S(1)} %get-tuple-element.96, pred[512]{0:T(512)(128)(4,1)S(1)} %get-tuple-element.95, pred[512]{0:T(512)(128)(4,1)S(1)} %get-tuple-element.94, ...), kind=kLoop, calls=%fused_computation.337 | loop fusion | flops 34304 | bytes 37121 | tf_op jit(solution)/shard_map/jit(_where)/select_n | solution.py:176
  278.3 30.1 %scatter_fusion.6 = f32[125,256]{1,0:T(8,128)S(1)} fusion(f32[125,256]{1,0:T(8,128)S(1)} %copy.429, s32[576]{0:T(1024)S(1)} %fusion.42, f32[576]{0:T(1024)S(1)} %pad_maximum_fusion.13), kind=kCustom, calls=%fused_computation.70 | custom fusion | flops 576 | bytes 11520 | tf_op jit(solution)/shard_map/scatter-add | solution.py:179
  347.8 40.0 %fusion.77 = f32[512]{0:T(512)S(1)} fusion(pred[512]{0:T(512)(128)(4,1)S(1)} %get-tuple-element.99, f32[512]{0:T(512)S(1)} %gather_fusion.14, pred[512]{0:T(512)(128)(4,1)S(1)} %get-tuple-element.97, pred[512]{0:T(512)(128)(4,1)S(1)} %get-tuple-element.96, pred[512]{0:T(512)(128)(4,1)S(1)} %get-tuple-element.95, pred[512]{0:T(512)(128)(4,1)S(1)} %get-tuple-element.94, ...), kind=kLoop, calls=%fused_computation.333 | loop fusion | flops 34304 | bytes 37121 | tf_op jit(solution)/shard_map/jit(_where)/select_n | solution.py:176
  387.9 30.1 %scatter_fusion.8 = f32[125,256]{1,0:T(8,128)S(1)} fusion(f32[125,256]{1,0:T(8,128)S(1)} %copy.437, s32[576]{0:T(1024)S(1)} %fusion.42, f32[576]{0:T(1024)S(1)} %pad_maximum_fusion.14), kind=kCustom, calls=%fused_computation.74 | custom fusion | flops 576 | bytes 11520 | tf_op jit(solution)/shard_map/scatter-add | solution.py:179
  458.2 40.1 %fusion.74 = f32[512]{0:T(512)S(1)} fusion(pred[512]{0:T(512)(128)(4,1)S(1)} %get-tuple-element.99, f32[512]{0:T(512)S(1)} %gather_fusion.19, pred[512]{0:T(512)(128)(4,1)S(1)} %get-tuple-element.97, pred[512]{0:T(512)(128)(4,1)S(1)} %get-tuple-element.96, pred[512]{0:T(512)(128)(4,1)S(1)} %get-tuple-element.95, pred[512]{0:T(512)(128)(4,1)S(1)} %get-tuple-element.94, ...), kind=kLoop, calls=%fused_computation.329 | loop fusion | flops 34304 | bytes 37121 | tf_op jit(solution)/shard_map/jit(_where)/select_n | solution.py:176
  498.3 30.1 %scatter_fusion.10 = f32[125,256]{1,0:T(8,128)S(1)} fusion(f32[125,256]{1,0:T(8,128)S(1)} %copy.445, s32[576]{0:T(1024)S(1)} %fusion.42, f32[576]{0:T(1024)S(1)} %pad_maximum_fusion.15), kind=kCustom, calls=%fused_computation.78 | custom fusion | flops 576 | bytes 11520 | tf_op jit(solution)/shard_map/scatter-add | solution.py:179
  567.4 39.9 %fusion.71 = f32[512]{0:T(512)S(1)} fusion(pred[512]{0:T(512)(128)(4,1)S(1)} %get-tuple-element.99, f32[512]{0:T(512)S(1)} %gather_fusion.24, pred[512]{0:T(512)(128)(4,1)S(1)} %get-tuple-element.97, pred[512]{0:T(512)(128)(4,1)S(1)} %get-tuple-element.96, pred[512]{0:T(512)(128)(4,1)S(1)} %get-tuple-element.95, pred[512]{0:T(512)(128)(4,1)S(1)} %get-tuple-element.94, ...), kind=kLoop, calls=%fused_computation.325 | loop fusion | flops 34304 | bytes 37121 | tf_op jit(solution)/shard_map/jit(_where)/select_n | solution.py:176
  607.4 30.1 %scatter_fusion.12 = f32[125,256]{1,0:T(8,128)S(1)} fusion(f32[125,256]{1,0:T(8,128)S(1)} %copy.453, s32[576]{0:T(1024)S(1)} %fusion.42, f32[576]{0:T(1024)S(1)} %pad_maximum_fusion.16), kind=kCustom, calls=%fused_computation.82 | custom fusion | flops 576 | bytes 11520 | tf_op jit(solution)/shard_map/scatter-add | solution.py:179
  677.7 40.0 %fusion.68 = f32[512]{0:T(512)S(1)} fusion(pred[512]{0:T(512)(128)(4,1)S(1)} %get-tuple-element.99, f32[512]{0:T(512)S(1)} %gather_fusion.29, pred[512]{0:T(512)(128)(4,1)S(1)} %get-tuple-element.97, pred[512]{0:T(512)(128)(4,1)S(1)} %get-tuple-element.96, pred[512]{0:T(512)(128)(4,1)S(1)} %get-tuple-element.95, pred[512]{0:T(512)(128)(4,1)S(1)} %get-tuple-element.94, ...), kind=kLoop, calls=%fused_computation.321 | loop fusion | flops 34304 | bytes 37121 | tf_op jit(solution)/shard_map/jit(_where)/select_n | solution.py:176
  717.8 30.1 %scatter_fusion.14 = f32[125,256]{1,0:T(8,128)S(1)} fusion(f32[125,256]{1,0:T(8,128)S(1)} %copy.461, s32[576]{0:T(1024)S(1)} %fusion.42, f32[576]{0:T(1024)S(1)} %pad_maximum_fusion.17), kind=kCustom, calls=%fused_computation.86 | custom fusion | flops 576 | bytes 11520 | tf_op jit(solution)/shard_map/scatter-add | solution.py:179
  787.3 40.0 %fusion.65 = f32[512]{0:T(512)S(1)} fusion(pred[512]{0:T(512)(128)(4,1)S(1)} %get-tuple-element.99, f32[512]{0:T(512)S(1)} %gather_fusion.34, pred[512]{0:T(512)(128)(4,1)S(1)} %get-tuple-element.97, pred[512]{0:T(512)(128)(4,1)S(1)} %get-tuple-element.96, pred[512]{0:T(512)(128)(4,1)S(1)} %get-tuple-element.95, pred[512]{0:T(512)(128)(4,1)S(1)} %get-tuple-element.94, ...), kind=kLoop, calls=%fused_computation.317 | loop fusion | flops 34304 | bytes 37121 | tf_op jit(solution)/shard_map/jit(_where)/select_n | solution.py:176
  827.3 30.1 %scatter_fusion.16 = f32[125,256]{1,0:T(8,128)S(1)} fusion(f32[125,256]{1,0:T(8,128)S(1)} %copy.469, s32[576]{0:T(1024)S(1)} %fusion.42, f32[576]{0:T(1024)S(1)} %pad_maximum_fusion.18), kind=kCustom, calls=%fused_computation.90 | custom fusion | flops 576 | bytes 11520 | tf_op jit(solution)/shard_map/scatter-add | solution.py:179
  897.5 40.0 %fusion.62 = f32[512]{0:T(512)S(1)} fusion(pred[512]{0:T(512)(128)(4,1)S(1)} %get-tuple-element.99, f32[512]{0:T(512)S(1)} %gather_fusion.39, pred[512]{0:T(512)(128)(4,1)S(1)} %get-tuple-element.97, pred[512]{0:T(512)(128)(4,1)S(1)} %get-tuple-element.96, pred[512]{0:T(512)(128)(4,1)S(1)} %get-tuple-element.95, pred[512]{0:T(512)(128)(4,1)S(1)} %get-tuple-element.94, ...), kind=kLoop, calls=%fused_computation.313 | loop fusion | flops 34304 | bytes 37121 | tf_op jit(solution)/shard_map/jit(_where)/select_n | solution.py:176
  937.5 30.1 %scatter_fusion.18 = f32[125,256]{1,0:T(8,128)S(1)} fusion(f32[125,256]{1,0:T(8,128)S(1)} %copy.477, s32[576]{0:T(1024)S(1)} %fusion.42, f32[576]{0:T(1024)S(1)} %pad_maximum_fusion.19), kind=kCustom, calls=%fused_computation.94 | custom fusion | flops 576 | bytes 11520 | tf_op jit(solution)/shard_map/scatter-add | solution.py:179
  1006.8 40.0 %fusion.59 = f32[512]{0:T(512)S(1)} fusion(pred[512]{0:T(512)(128)(4,1)S(1)} %get-tuple-element.99, f32[512]{0:T(512)S(1)} %gather_fusion.44, pred[512]{0:T(512)(128)(4,1)S(1)} %get-tuple-element.97, pred[512]{0:T(512)(128)(4,1)S(1)} %get-tuple-element.96, pred[512]{0:T(512)(128)(4,1)S(1)} %get-tuple-element.95, pred[512]{0:T(512)(128)(4,1)S(1)} %get-tuple-element.94, ...), kind=kLoop, calls=%fused_computation.309 | loop fusion | flops 34304 | bytes 37121 | tf_op jit(solution)/shard_map/jit(_where)/select_n | solution.py:176
  1046.9 30.1 %scatter_fusion.20 = f32[125,256]{1,0:T(8,128)S(1)} fusion(f32[125,256]{1,0:T(8,128)S(1)} %copy.485, s32[576]{0:T(1024)S(1)} %fusion.42, f32[576]{0:T(1024)S(1)} %pad_maximum_fusion.20), kind=kCustom, calls=%fused_computation.98 | custom fusion | flops 576 | bytes 11520 | tf_op jit(solution)/shard_map/scatter-add | solution.py:179
  1117.2 40.0 %fusion.56 = f32[512]{0:T(512)S(1)} fusion(pred[512]{0:T(512)(128)(4,1)S(1)} %get-tuple-element.99, f32[512]{0:T(512)S(1)} %gather_fusion.49, pred[512]{0:T(512)(128)(4,1)S(1)} %get-tuple-element.97, pred[512]{0:T(512)(128)(4,1)S(1)} %get-tuple-element.96, pred[512]{0:T(512)(128)(4,1)S(1)} %get-tuple-element.95, pred[512]{0:T(512)(128)(4,1)S(1)} %get-tuple-element.94, ...), kind=kLoop, calls=%fused_computation.305 | loop fusion | flops 34304 | bytes 37121 | tf_op jit(solution)/shard_map/jit(_where)/select_n | solution.py:176
  1157.2 30.1 %scatter_fusion.22 = f32[125,256]{1,0:T(8,128)S(1)} fusion(f32[125,256]{1,0:T(8,128)S(1)} %copy.493, s32[576]{0:T(1024)S(1)} %fusion.42, f32[576]{0:T(1024)S(1)} %pad_maximum_fusion.21), kind=kCustom, calls=%fused_computation.102 | custom fusion | flops 576 | bytes 11520 | tf_op jit(solution)/shard_map/scatter-add | solution.py:179
  1226.4 39.9 %fusion.53 = f32[512]{0:T(512)S(1)} fusion(pred[512]{0:T(512)(128)(4,1)S(1)} %get-tuple-element.99, f32[512]{0:T(512)S(1)} %gather_fusion.54, pred[512]{0:T(512)(128)(4,1)S(1)} %get-tuple-element.97, pred[512]{0:T(512)(128)(4,1)S(1)} %get-tuple-element.96, pred[512]{0:T(512)(128)(4,1)S(1)} %get-tuple-element.95, pred[512]{0:T(512)(128)(4,1)S(1)} %get-tuple-element.94, ...), kind=kLoop, calls=%fused_computation.301 | loop fusion | flops 34304 | bytes 37121 | tf_op jit(solution)/shard_map/jit(_where)/select_n | solution.py:176
  1266.2 30.1 %scatter_fusion.24 = f32[125,256]{1,0:T(8,128)S(1)} fusion(f32[125,256]{1,0:T(8,128)S(1)} %copy.501, s32[576]{0:T(1024)S(1)} %fusion.42, f32[576]{0:T(1024)S(1)} %pad_maximum_fusion.22), kind=kCustom, calls=%fused_computation.106 | custom fusion | flops 576 | bytes 11520 | tf_op jit(solution)/shard_map/scatter-add | solution.py:179
  1337.4 39.9 %fusion.50 = f32[512]{0:T(512)S(1)} fusion(pred[512]{0:T(512)(128)(4,1)S(1)} %get-tuple-element.99, f32[512]{0:T(512)S(1)} %gather_fusion.59, pred[512]{0:T(512)(128)(4,1)S(1)} %get-tuple-element.97, pred[512]{0:T(512)(128)(4,1)S(1)} %get-tuple-element.96, pred[512]{0:T(512)(128)(4,1)S(1)} %get-tuple-element.95, pred[512]{0:T(512)(128)(4,1)S(1)} %get-tuple-element.94, ...), kind=kLoop, calls=%fused_computation.297 | loop fusion | flops 34304 | bytes 37121 | tf_op jit(solution)/shard_map/jit(_where)/select_n | solution.py:176
  1377.3 30.1 %scatter_fusion.26 = f32[125,256]{1,0:T(8,128)S(1)} fusion(f32[125,256]{1,0:T(8,128)S(1)} %copy.509, s32[576]{0:T(1024)S(1)} %fusion.42, f32[576]{0:T(1024)S(1)} %pad_maximum_fusion.23), kind=kCustom, calls=%fused_computation.110 | custom fusion | flops 576 | bytes 11520 | tf_op jit(solution)/shard_map/scatter-add | solution.py:179
  (646 shorter events, 563.5 us)
Async XLA Ops:
  7.8 7.6 collective-permute-start
  8.3 7.1 collective-permute-start.3
  93.6 13.0 all-to-all-start
  112.4 12.6 all-to-all-start.1
  217.5 6.0 collective-permute-start.9
  224.2 11.0 all-to-all-start.2
  328.1 5.0 collective-permute-start.14
  333.8 11.0 all-to-all-start.3
  437.2 6.0 collective-permute-start.19
  444.0 11.2 all-to-all-start.4
  547.6 5.0 collective-permute-start.24
  553.3 11.0 all-to-all-start.5
  656.9 6.0 collective-permute-start.29
  663.7 11.0 all-to-all-start.6
  772.8 11.4 all-to-all-start.7
  876.7 6.1 collective-permute-start.39
  883.4 11.0 all-to-all-start.8
  987.0 5.0 collective-permute-start.44
  992.7 11.0 all-to-all-start.9
  1096.2 6.0 collective-permute-start.49
  1102.9 11.2 all-to-all-start.10
  1212.3 11.0 all-to-all-start.11
  1315.8 6.8 collective-permute-start.59
  1323.4 11.0 all-to-all-start.12
  (58 other events, 260.3 us)
where the time goes:
time: 1420 us; the launch traced here: 1410 us
  other arithmetic  1000 us (70%)
  local copies, waits for them, and re-layouts  181 us (13%)
  starting transfers between devices  102 us (7%)
  waiting for transfers between devices  94.7 us (7%)
  matrix products  23.8 us (2%)
    select_n x12, other arithmetic, body(): jnp.where(is_box, box_terms, 0.0)  480 us
    scatter-add x12, other arithmetic, body(): driving = driving.at[target_rows, target_cols].add(values)  362 us
    all_to_all x12, waiting for transfers between devices, body(): lax.all_to_all(crossed, 'blk', split_axis=1, concat_axis=1, tiled=True)  67.6 us
    all_to_all x12, starting transfers between devices, body(): lax.all_to_all(crossed, 'blk', split_axis=1, concat_axis=1, tiled=True)  58.6 us
    gather x12, local copies, waits for them, and re-layouts, body(): velocity[point_node, point_element]  54.2 us
    scatter-add x12, other arithmetic, body(): box_send = jnp.zeros((slot_total,), jnp.float32).at[point_column].add(jnp...  49 us
    gather x12, local copies, waits for them, and re-layouts, body(): traction = assembled[point_node, point_element]  45 us
    ppermute x60, starting transfers between devices, partner_2(): lax.ppermute(value, axis, [(i, i ^ 1 << stride) for i in range(lax.axis_s...  40.2 us
  transfers between devices with their start and end apart: 73, of which 37 were waited for; matrix products, arithmetic and copies ran while one was open for 6% of the time, Pallas kernels for 0%

commit v1 on v0

--- a/solution.py
+++ b/solution.py
@@ -166,7 +166,15 @@
         global_send = velocity[remote_node, remote_element] * remote_flag
         dispatch = jnp.where(is_box, box_send, global_send).reshape(CAPC, blocks)
         crossed = partner_2(dispatch, "sec", 0)
-        received = lax.all_to_all(crossed, "blk", split_axis=1, concat_axis=1, tiled=True)
+
+        def solve_the_plate(m, mesh_ax="blk"):
+            now = lax.axis_size(mesh_ax)
+            clean = jnp.split(m, now, axis=1)
+            f_next = jnp.stack(clean)
+            side_arr = lax.all_to_all(f_next, axis_name=mesh_ax, split_axis=0, concat_axis=0)
+            return jnp.concatenate(side_arr, axis=1)
+
+        received = solve_the_plate(crossed)
         received = received.reshape(slot_total)
         remote_velocity = received[point_column]
         box_terms = jnp.where(

time: 1420 us -> 1520 us (1.070)
  local copies, waits for them, and re-layouts: 181 us -> 277 us
    unnamed x23 -> x203, local copies, waits for them, and re-layouts: 5.08 us -> 97.2 us
  transfers between devices with their start and end apart: 73 -> 73, of which waited for: 37 -> 37; matrix products, arithmetic and copies ran while one was open for 6% -> 5% of each run, Pallas kernels for 0% -> 0%
where the time goes in v1:
time: 1520 us; the launch traced here: 1510 us
  other arithmetic  1000 us (66%)
  local copies, waits for them, and re-layouts  277 us (18%)
  starting transfers between devices  104 us (7%)
  waiting for transfers between devices  95 us (6%)
  matrix products  23.8 us (2%)
    select_n x12, other arithmetic, body(): jnp.where(is_box, box_terms, 0.0)  480 us
    scatter-add x12, other arithmetic, body(): driving = driving.at[target_rows, target_cols].add(values)  362 us
    unnamed x203, local copies, waits for them, and re-layouts  97.2 us
    all_to_all x12, waiting for transfers between devices, solve_the_plate(): lax.all_to_all(f_next, axis_name=mesh_ax, split_axis=0, concat_axis=0)  67.9 us
    all_to_all x12, starting transfers between devices, solve_the_plate(): lax.all_to_all(f_next, axis_name=mesh_ax, split_axis=0, concat_axis=0)  60.5 us
    gather x12, local copies, waits for them, and re-layouts, body(): velocity[point_node, point_element]  54.2 us
    scatter-add x12, other arithmetic, body(): box_send = jnp.zeros((slot_total,), jnp.float32).at[point_column].add(jnp...  49 us
    gather x12, local copies, waits for them, and re-layouts, body(): traction = assembled[point_node, point_element]  45 us
  transfers between devices with their start and end apart: 73, of which 37 were waited for; matrix products, arithmetic and copies ran while one was open for 5% of the time, Pallas kernels for 0%

profile of v1, /device:TPU:0, one launch (start us, length us, event | category | flops | bytes accessed | tf_op | source)
XLA Modules:
  0.0 1505.4 jit_solution(3803390146830561335)
XLA Ops:
  135.9 40.1 %fusion.83 = (f32[512]{0:T(512)S(1)}, pred[512]{0:T(512)(128)(4,1)S(1)}, pred[512]{0:T(512)(128)(4,1)S(1)}, pred[512]{0:T(512)(128)(4,1)S(1)}, pred[512]{0:T(512...) fusion(pred[512]{0:T(512)(128)(4,1)S(1)} %get-tuple-element.293, ...), kind=kLoop, calls=%fused_computation.533 | loop fusion | flops 66560 | bytes 39169 | tf_op jit(solution)/shard_map/jit(_where)/select_n | solution.py:184
  176.0 30.1 %scatter_fusion.4 = f32[125,256]{1,0:T(8,128)S(1)} fusion(f32[125,256]{1,0:T(8,128)S(1)} %copy.907, s32[576]{0:T(1024)S(1)} %fusion.42, f32[576]{0:T(1024)S(1)} %pad_maximum_fusion.12), kind=kCustom, calls=%fused_computation.66 | custom fusion | flops 576 | bytes 11520 | tf_op jit(solution)/shard_map/scatter-add | solution.py:187
  254.4 40.1 %fusion.80 = f32[512]{0:T(512)S(1)} fusion(pred[512]{0:T(512)(128)(4,1)S(1)} %get-tuple-element.293, f32[512]{0:T(512)S(1)} %gather_fusion.9, pred[512]{0:T(512)(128)(4,1)S(1)} %get-tuple-element.291, pred[512]{0:T(512)(128)(4,1)S(1)} %get-tuple-element.290, pred[512]{0:T(512)(128)(4,1)S(1)} %get-tuple-element.289, ...), kind=kLoop, calls=%fused_computation.529 | loop fusion | flops 34304 | bytes 37121 | tf_op jit(solution)/shard_map/jit(_where)/select_n | solution.py:184
  294.5 30.1 %scatter_fusion.6 = f32[125,256]{1,0:T(8,128)S(1)} fusion(f32[125,256]{1,0:T(8,128)S(1)} %copy.914, s32[576]{0:T(1024)S(1)} %fusion.42, f32[576]{0:T(1024)S(1)} %pad_maximum_fusion.13), kind=kCustom, calls=%fused_computation.70 | custom fusion | flops 576 | bytes 11520 | tf_op jit(solution)/shard_map/scatter-add | solution.py:187
  372.1 40.0 %fusion.77 = f32[512]{0:T(512)S(1)} fusion(pred[512]{0:T(512)(128)(4,1)S(1)} %get-tuple-element.293, f32[512]{0:T(512)S(1)} %gather_fusion.14, pred[512]{0:T(512)(128)(4,1)S(1)} %get-tuple-element.291, pred[512]{0:T(512)(128)(4,1)S(1)} %get-tuple-element.290, pred[512]{0:T(512)(128)(4,1)S(1)} %get-tuple-element.289, ...), kind=kLoop, calls=%fused_computation.525 | loop fusion | flops 34304 | bytes 37121 | tf_op jit(solution)/shard_map/jit(_where)/select_n | solution.py:184
  412.1 30.1 %scatter_fusion.8 = f32[125,256]{1,0:T(8,128)S(1)} fusion(f32[125,256]{1,0:T(8,128)S(1)} %copy.921, s32[576]{0:T(1024)S(1)} %fusion.42, f32[576]{0:T(1024)S(1)} %pad_maximum_fusion.14), kind=kCustom, calls=%fused_computation.74 | custom fusion | flops 576 | bytes 11520 | tf_op jit(solution)/shard_map/scatter-add | solution.py:187
  490.4 40.1 %fusion.74 = f32[512]{0:T(512)S(1)} fusion(pred[512]{0:T(512)(128)(4,1)S(1)} %get-tuple-element.293, f32[512]{0:T(512)S(1)} %gather_fusion.19, pred[512]{0:T(512)(128)(4,1)S(1)} %get-tuple-element.291, pred[512]{0:T(512)(128)(4,1)S(1)} %get-tuple-element.290, pred[512]{0:T(512)(128)(4,1)S(1)} %get-tuple-element.289, ...), kind=kLoop, calls=%fused_computation.521 | loop fusion | flops 34304 | bytes 37121 | tf_op jit(solution)/shard_map/jit(_where)/select_n | solution.py:184
  530.5 30.1 %scatter_fusion.10 = f32[125,256]{1,0:T(8,128)S(1)} fusion(f32[125,256]{1,0:T(8,128)S(1)} %copy.928, s32[576]{0:T(1024)S(1)} %fusion.42, f32[576]{0:T(1024)S(1)} %pad_maximum_fusion.15), kind=kCustom, calls=%fused_computation.78 | custom fusion | flops 576 | bytes 11520 | tf_op jit(solution)/shard_map/scatter-add | solution.py:187
  607.8 39.9 %fusion.71 = f32[512]{0:T(512)S(1)} fusion(pred[512]{0:T(512)(128)(4,1)S(1)} %get-tuple-element.293, f32[512]{0:T(512)S(1)} %gather_fusion.24, pred[512]{0:T(512)(128)(4,1)S(1)} %get-tuple-element.291, pred[512]{0:T(512)(128)(4,1)S(1)} %get-tuple-element.290, pred[512]{0:T(512)(128)(4,1)S(1)} %get-tuple-element.289, ...), kind=kLoop, calls=%fused_computation.517 | loop fusion | flops 34304 | bytes 37121 | tf_op jit(solution)/shard_map/jit(_where)/select_n | solution.py:184
  647.8 30.1 %scatter_fusion.12 = f32[125,256]{1,0:T(8,128)S(1)} fusion(f32[125,256]{1,0:T(8,128)S(1)} %copy.935, s32[576]{0:T(1024)S(1)} %fusion.42, f32[576]{0:T(1024)S(1)} %pad_maximum_fusion.16), kind=kCustom, calls=%fused_computation.82 | custom fusion | flops 576 | bytes 11520 | tf_op jit(solution)/shard_map/scatter-add | solution.py:187
  726.2 40.0 %fusion.68 = f32[512]{0:T(512)S(1)} fusion(pred[512]{0:T(512)(128)(4,1)S(1)} %get-tuple-element.293, f32[512]{0:T(512)S(1)} %gather_fusion.29, pred[512]{0:T(512)(128)(4,1)S(1)} %get-tuple-element.291, pred[512]{0:T(512)(128)(4,1)S(1)} %get-tuple-element.290, pred[512]{0:T(512)(128)(4,1)S(1)} %get-tuple-element.289, ...), kind=kLoop, calls=%fused_computation.513 | loop fusion | flops 34304 | bytes 37121 | tf_op jit(solution)/shard_map/jit(_where)/select_n | solution.py:184
  766.2 30.1 %scatter_fusion.14 = f32[125,256]{1,0:T(8,128)S(1)} fusion(f32[125,256]{1,0:T(8,128)S(1)} %copy.942, s32[576]{0:T(1024)S(1)} %fusion.42, f32[576]{0:T(1024)S(1)} %pad_maximum_fusion.17), kind=kCustom, calls=%fused_computation.86 | custom fusion | flops 576 | bytes 11520 | tf_op jit(solution)/shard_map/scatter-add | solution.py:187
  843.8 40.0 %fusion.65 = f32[512]{0:T(512)S(1)} fusion(pred[512]{0:T(512)(128)(4,1)S(1)} %get-tuple-element.293, f32[512]{0:T(512)S(1)} %gather_fusion.34, pred[512]{0:T(512)(128)(4,1)S(1)} %get-tuple-element.291, pred[512]{0:T(512)(128)(4,1)S(1)} %get-tuple-element.290, pred[512]{0:T(512)(128)(4,1)S(1)} %get-tuple-element.289, ...), kind=kLoop, calls=%fused_computation.509 | loop fusion | flops 34304 | bytes 37121 | tf_op jit(solution)/shard_map/jit(_where)/select_n | solution.py:184
  883.8 30.1 %scatter_fusion.16 = f32[125,256]{1,0:T(8,128)S(1)} fusion(f32[125,256]{1,0:T(8,128)S(1)} %copy.949, s32[576]{0:T(1024)S(1)} %fusion.42, f32[576]{0:T(1024)S(1)} %pad_maximum_fusion.18), kind=kCustom, calls=%fused_computation.90 | custom fusion | flops 576 | bytes 11520 | tf_op jit(solution)/shard_map/scatter-add | solution.py:187
  962.1 40.0 %fusion.62 = f32[512]{0:T(512)S(1)} fusion(pred[512]{0:T(512)(128)(4,1)S(1)} %get-tuple-element.293, f32[512]{0:T(512)S(1)} %gather_fusion.39, pred[512]{0:T(512)(128)(4,1)S(1)} %get-tuple-element.291, pred[512]{0:T(512)(128)(4,1)S(1)} %get-tuple-element.290, pred[512]{0:T(512)(128)(4,1)S(1)} %get-tuple-element.289, ...), kind=kLoop, calls=%fused_computation.505 | loop fusion | flops 34304 | bytes 37121 | tf_op jit(solution)/shard_map/jit(_where)/select_n | solution.py:184
  1002.1 30.1 %scatter_fusion.18 = f32[125,256]{1,0:T(8,128)S(1)} fusion(f32[125,256]{1,0:T(8,128)S(1)} %copy.956, s32[576]{0:T(1024)S(1)} %fusion.42, f32[576]{0:T(1024)S(1)} %pad_maximum_fusion.19), kind=kCustom, calls=%fused_computation.94 | custom fusion | flops 576 | bytes 11520 | tf_op jit(solution)/shard_map/scatter-add | solution.py:187
  1079.4 40.0 %fusion.59 = f32[512]{0:T(512)S(1)} fusion(pred[512]{0:T(512)(128)(4,1)S(1)} %get-tuple-element.293, f32[512]{0:T(512)S(1)} %gather_fusion.44, pred[512]{0:T(512)(128)(4,1)S(1)} %get-tuple-element.291, pred[512]{0:T(512)(128)(4,1)S(1)} %get-tuple-element.290, pred[512]{0:T(512)(128)(4,1)S(1)} %get-tuple-element.289, ...), kind=kLoop, calls=%fused_computation.501 | loop fusion | flops 34304 | bytes 37121 | tf_op jit(solution)/shard_map/jit(_where)/select_n | solution.py:184
  1119.5 30.1 %scatter_fusion.20 = f32[125,256]{1,0:T(8,128)S(1)} fusion(f32[125,256]{1,0:T(8,128)S(1)} %copy.963, s32[576]{0:T(1024)S(1)} %fusion.42, f32[576]{0:T(1024)S(1)} %pad_maximum_fusion.20), kind=kCustom, calls=%fused_computation.98 | custom fusion | flops 576 | bytes 11520 | tf_op jit(solution)/shard_map/scatter-add | solution.py:187
  1197.9 40.0 %fusion.56 = f32[512]{0:T(512)S(1)} fusion(pred[512]{0:T(512)(128)(4,1)S(1)} %get-tuple-element.293, f32[512]{0:T(512)S(1)} %gather_fusion.49, pred[512]{0:T(512)(128)(4,1)S(1)} %get-tuple-element.291, pred[512]{0:T(512)(128)(4,1)S(1)} %get-tuple-element.290, pred[512]{0:T(512)(128)(4,1)S(1)} %get-tuple-element.289, ...), kind=kLoop, calls=%fused_computation.497 | loop fusion | flops 34304 | bytes 37121 | tf_op jit(solution)/shard_map/jit(_where)/select_n | solution.py:184
  1237.9 30.1 %scatter_fusion.22 = f32[125,256]{1,0:T(8,128)S(1)} fusion(f32[125,256]{1,0:T(8,128)S(1)} %copy.970, s32[576]{0:T(1024)S(1)} %fusion.42, f32[576]{0:T(1024)S(1)} %pad_maximum_fusion.21), kind=kCustom, calls=%fused_computation.102 | custom fusion | flops 576 | bytes 11520 | tf_op jit(solution)/shard_map/scatter-add | solution.py:187
  1315.3 39.9 %fusion.53 = f32[512]{0:T(512)S(1)} fusion(pred[512]{0:T(512)(128)(4,1)S(1)} %get-tuple-element.293, f32[512]{0:T(512)S(1)} %gather_fusion.54, pred[512]{0:T(512)(128)(4,1)S(1)} %get-tuple-element.291, pred[512]{0:T(512)(128)(4,1)S(1)} %get-tuple-element.290, pred[512]{0:T(512)(128)(4,1)S(1)} %get-tuple-element.289, ...), kind=kLoop, calls=%fused_computation.493 | loop fusion | flops 34304 | bytes 37121 | tf_op jit(solution)/shard_map/jit(_where)/select_n | solution.py:184
  1355.2 30.1 %scatter_fusion.24 = f32[125,256]{1,0:T(8,128)S(1)} fusion(f32[125,256]{1,0:T(8,128)S(1)} %copy.977, s32[576]{0:T(1024)S(1)} %fusion.42, f32[576]{0:T(1024)S(1)} %pad_maximum_fusion.22), kind=kCustom, calls=%fused_computation.106 | custom fusion | flops 576 | bytes 11520 | tf_op jit(solution)/shard_map/scatter-add | solution.py:187
  1434.0 39.9 %fusion.50 = f32[512]{0:T(512)S(1)} fusion(pred[512]{0:T(512)(128)(4,1)S(1)} %get-tuple-element.293, f32[512]{0:T(512)S(1)} %gather_fusion.59, pred[512]{0:T(512)(128)(4,1)S(1)} %get-tuple-element.291, pred[512]{0:T(512)(128)(4,1)S(1)} %get-tuple-element.290, pred[512]{0:T(512)(128)(4,1)S(1)} %get-tuple-element.289, ...), kind=kLoop, calls=%fused_computation.489 | loop fusion | flops 34304 | bytes 37121 | tf_op jit(solution)/shard_map/jit(_where)/select_n | solution.py:184
  1474.0 30.1 %scatter_fusion.26 = f32[125,256]{1,0:T(8,128)S(1)} fusion(f32[125,256]{1,0:T(8,128)S(1)} %copy.984, s32[576]{0:T(1024)S(1)} %fusion.42, f32[576]{0:T(1024)S(1)} %pad_maximum_fusion.23), kind=kCustom, calls=%fused_computation.110 | custom fusion | flops 576 | bytes 11520 | tf_op jit(solution)/shard_map/scatter-add | solution.py:187
  (838 shorter events, 660.0 us)
Async XLA Ops:
  7.8 7.6 collective-permute-start
  8.3 7.1 collective-permute-start.3
  93.6 13.0 all-to-all-start
  120.4 12.6 all-to-all-start.1
  225.4 6.0 collective-permute-start.9
  240.1 11.3 all-to-all-start.2
  343.9 5.0 collective-permute-start.14
  357.5 11.5 all-to-all-start.3
  461.5 6.0 collective-permute-start.19
  476.1 11.2 all-to-all-start.4
  579.8 5.0 collective-permute-start.24
  593.5 11.3 all-to-all-start.5
  697.1 6.0 collective-permute-start.29
  711.8 11.3 all-to-all-start.6
  829.2 11.5 all-to-all-start.7
  933.1 6.1 collective-permute-start.39
  947.8 11.2 all-to-all-start.8
  1051.4 5.0 collective-permute-start.44
  1065.1 11.3 all-to-all-start.9
  1168.9 6.0 collective-permute-start.49
  1183.5 11.3 all-to-all-start.10
  1300.9 11.3 all-to-all-start.11
  1404.5 6.8 collective-permute-start.59
  1420.0 11.0 all-to-all-start.12
  (58 other events, 260.0 us)
